TPU v7x, 32 devices: a whole 2x2x4 slice. The times are simulated.
32 devices in a mesh: dp: 8 (over z, x), fsdp: 4 (over y, core).
Axes of the slice: x: 2, y: 2, z: 4, core: 2. Of those that a mesh axis runs over, the one named last changes fastest.
Arguments:
- tokens: bfloat16 [64, 512, 768], P(('dp', 'fsdp')), may hold values from -6 to 6
- segments: int32 [64, 512], P(('dp', 'fsdp')), may hold values from 0 to 11, never falling along the last dimension, each value on 1 to 256 neighbouring positions
- w_query: bfloat16 [768, 768], P(('dp', 'fsdp')), may hold values from -0.21875 to 0.21875
- w_key: bfloat16 [768, 768], P(('dp', 'fsdp')), may hold values from -0.21875 to 0.21875
- w_value: bfloat16 [768, 768], P(('dp', 'fsdp')), may hold values from -0.21875 to 0.21875
- w_output: bfloat16 [768, 768], P(('dp', 'fsdp')), may hold values from -1.25 to 1.25
- w_inner: bfloat16 [768, 3072], P(('dp', 'fsdp')), may hold values from -0.21875 to 0.21875
- w_outer: bfloat16 [3072, 768], P(('dp', 'fsdp')), may hold values from -0.109375 to 0.109375
- down_query: bfloat16 [768, 8], P(('dp', 'fsdp')), may hold values from -0.21875 to 0.21875
- down_value: bfloat16 [768, 8], P(('dp', 'fsdp')), may hold values from -0.21875 to 0.21875
- up_query: bfloat16 [8, 768], replicated, may hold values from -0.59765625 to 0.59765625
- up_value: bfloat16 [8, 768], replicated, may hold values from -0.59765625 to 0.59765625
- norm1_gain: float32 [768], replicated, may hold values from 0.5 to 1.5
- norm1_shift: float32 [768], replicated, may hold values from -1.5 to 1.5
- norm2_gain: float32 [768], replicated, may hold values from 0.5 to 1.5
- norm2_shift: float32 [768], replicated, may hold values from -1.5 to 1.5
- out_grad: bfloat16 [64, 512, 768], P(('dp', 'fsdp')), may hold values from -6 to 6
Outputs:
- layer_out: bfloat16 [64, 512, 768], P(('dp', 'fsdp'))
- tokens_grad: bfloat16 [64, 512, 768], P(('dp', 'fsdp'))
- up_query_grad: float32 [8, 768], replicated
- up_value_grad: float32 [8, 768], replicated
Inputs may be any that keep to these rules, and one draw needn't show every extreme that they name: `segments`: within each packed row the segment numbers never fall; each item spans 1 to 256 positions, and some item spans exactly 256.
All inputs are finite; a program needn't handle non-finite values.
Results may differ from a plain program's by a relative error of at most 0.014.
The roundings to bfloat16 on the way count: a program that leaves them out, or rounds other values in their place, can miss the bound.
Values may be sent and summed in bfloat16 or wider, within the bound.
A program may use at most 128 MiB of HBM per device.

v0:
```python
import jax
import jax.numpy as jnp
from jax import lax
from jax.sharding import PartitionSpec as P

H = 12
HD = 64


def gelu_exact(values):
    return jax.nn.gelu(values, approximate=False)


def normalize(values):
    center = values - jnp.mean(values, axis=-1, keepdims=True)
    scaler = lax.rsqrt(jnp.mean(center * center, axis=-1, keepdims=True) + 1e-05)
    return (center * scaler, scaler)


def norm_back(grad_normed, normed, scaler):
    first = jnp.mean(grad_normed, axis=-1, keepdims=True)
    second = jnp.mean(grad_normed * normed, axis=-1, keepdims=True)
    return scaler * (grad_normed - first - normed * second)


def row_scores(q_row, k_row, seg_row):
    same = seg_row[:, None] == seg_row[None, :]
    scores = jnp.einsum("qhd,khd->hqk", q_row, k_row, preferred_element_type=jnp.float32) * 0.125
    return jnp.where(same[None], scores, -1e30)


def body(
    tokens,
    segments,
    w_query,
    w_key,
    w_value,
    w_output,
    w_inner,
    w_outer,
    down_query,
    down_value,
    up_query,
    up_value,
    norm1_gain,
    norm1_shift,
    norm2_gain,
    norm2_shift,
    out_grad,
):
    row_count, length, width = tokens.shape
    count = row_count * length
    whole = (
        lax.all_gather(w_query, ("dp", "fsdp"), axis=0, tiled=True),
        lax.all_gather(w_key, ("dp", "fsdp"), axis=0, tiled=True),
        lax.all_gather(w_value, ("dp", "fsdp"), axis=0, tiled=True),
        lax.all_gather(w_output, ("dp", "fsdp"), axis=0, tiled=True),
        lax.all_gather(w_inner, ("dp", "fsdp"), axis=0, tiled=True),
        lax.all_gather(w_outer, ("dp", "fsdp"), axis=0, tiled=True),
        lax.all_gather(down_query, ("dp", "fsdp"), axis=0, tiled=True),
        lax.all_gather(down_value, ("dp", "fsdp"), axis=0, tiled=True),
    )
    wq, wk, wv, wo, win, wout, dq_mat, dv_mat = whole
    tok_rows = tokens.reshape(count, width)
    low_q = jnp.dot(tok_rows, dq_mat, preferred_element_type=jnp.float32).astype(jnp.bfloat16)
    low_v = jnp.dot(tok_rows, dv_mat, preferred_element_type=jnp.float32).astype(jnp.bfloat16)
    queries = (
        jnp.dot(tok_rows, wq, preferred_element_type=jnp.float32)
        + 2.0 * jnp.dot(low_q, up_query, preferred_element_type=jnp.float32)
    ).astype(jnp.bfloat16)
    keys_all = jnp.dot(tok_rows, wk, preferred_element_type=jnp.float32).astype(jnp.bfloat16)
    values_all = (
        jnp.dot(tok_rows, wv, preferred_element_type=jnp.float32)
        + 2.0 * jnp.dot(low_v, up_value, preferred_element_type=jnp.float32)
    ).astype(jnp.bfloat16)
    q_heads = queries.reshape(row_count, length, H, HD)
    k_heads = keys_all.reshape(row_count, length, H, HD)
    v_heads = values_all.reshape(row_count, length, H, HD)

    def attend(items):
        q_row, k_row, v_row, seg_row = items
        masked = row_scores(q_row, k_row, seg_row)
        highest = jnp.max(masked, axis=-1, keepdims=True)
        expos = jnp.exp(masked - highest)
        totals = jnp.sum(expos, axis=-1, keepdims=True)
        probs = (expos / totals).astype(jnp.bfloat16)
        context = jnp.einsum("hqk,khd->qhd", probs, v_row, preferred_element_type=jnp.float32)
        return (context.astype(jnp.bfloat16), highest + jnp.log(totals))

    contexts, log_totals = lax.map(attend, (q_heads, k_heads, v_heads, segments))
    context_rows = contexts.reshape(count, width)
    summed1 = tok_rows.astype(jnp.float32) + jnp.dot(
        context_rows, wo, preferred_element_type=jnp.float32
    )
    normed1, scaler1 = normalize(summed1)
    hidden1 = normed1 * norm1_gain + norm1_shift
    hidden_low = hidden1.astype(jnp.bfloat16)
    inner = jnp.dot(hidden_low, win, preferred_element_type=jnp.float32)
    active = gelu_exact(inner).astype(jnp.bfloat16)
    summed2 = hidden1 + jnp.dot(active, wout, preferred_element_type=jnp.float32)
    normed2, scaler2 = normalize(summed2)
    layer_out = (normed2 * norm2_gain + norm2_shift).astype(jnp.bfloat16)
    second = (
        lax.all_gather(w_query, ("dp", "fsdp"), axis=0, tiled=True),
        lax.all_gather(w_key, ("dp", "fsdp"), axis=0, tiled=True),
        lax.all_gather(w_value, ("dp", "fsdp"), axis=0, tiled=True),
        lax.all_gather(w_output, ("dp", "fsdp"), axis=0, tiled=True),
        lax.all_gather(w_inner, ("dp", "fsdp"), axis=0, tiled=True),
        lax.all_gather(w_outer, ("dp", "fsdp"), axis=0, tiled=True),
        lax.all_gather(down_query, ("dp", "fsdp"), axis=0, tiled=True),
        lax.all_gather(down_value, ("dp", "fsdp"), axis=0, tiled=True),
    )
    wq, wk, wv, wo, win, wout, dq_mat, dv_mat = second
    cotangent = out_grad.reshape(count, width).astype(jnp.float32)
    grad_sum2 = norm_back(cotangent * norm2_gain, normed2, scaler2)
    grad_branch = grad_sum2.astype(jnp.bfloat16)
    inner_again = jnp.dot(hidden_low, win, preferred_element_type=jnp.float32)
    gelu_value, gelu_pull = jax.vjp(gelu_exact, inner_again)
    grad_active = jnp.dot(grad_branch, wout.T, preferred_element_type=jnp.float32)
    grad_inner = gelu_pull(grad_active)[0].astype(jnp.bfloat16)
    grad_hidden = grad_sum2 + jnp.dot(grad_inner, win.T, preferred_element_type=jnp.float32)
    grad_sum1 = norm_back(grad_hidden * norm1_gain, normed1, scaler1)
    grad_attended = grad_sum1.astype(jnp.bfloat16)
    grad_context = jnp.dot(grad_attended, wo.T, preferred_element_type=jnp.float32).astype(
        jnp.bfloat16
    )
    grad_heads = grad_context.reshape(row_count, length, H, HD)

    def attend_back(items):
        q_row, k_row, v_row, seg_row, lse_row, grad_row = items
        masked = row_scores(q_row, k_row, seg_row)
        probs = jnp.exp(masked - lse_row)
        grad_v = jnp.einsum(
            "hqk,qhd->khd", probs.astype(jnp.bfloat16), grad_row, preferred_element_type=jnp.float32
        )
        grad_probs = jnp.einsum("qhd,khd->hqk", grad_row, v_row, preferred_element_type=jnp.float32)
        inner_sum = jnp.sum(grad_probs * probs, axis=-1, keepdims=True)
        grad_scores = (probs * (grad_probs - inner_sum)).astype(jnp.bfloat16)
        grad_q = (
            jnp.einsum("hqk,khd->qhd", grad_scores, k_row, preferred_element_type=jnp.float32)
            * 0.125
        )
        grad_k = (
            jnp.einsum("hqk,qhd->khd", grad_scores, q_row, preferred_element_type=jnp.float32)
            * 0.125
        )
        return (
            grad_q.astype(jnp.bfloat16),
            grad_k.astype(jnp.bfloat16),
            grad_v.astype(jnp.bfloat16),
        )

    grad_qh, grad_kh, grad_vh = lax.map(
        attend_back, (q_heads, k_heads, v_heads, segments, log_totals, grad_heads)
    )
    grad_query = grad_qh.reshape(count, width)
    grad_key = grad_kh.reshape(count, width)
    grad_value = grad_vh.reshape(count, width)
    grad_low_q = (2.0 * jnp.dot(grad_query, up_query.T, preferred_element_type=jnp.float32)).astype(
        jnp.bfloat16
    )
    grad_low_v = (2.0 * jnp.dot(grad_value, up_value.T, preferred_element_type=jnp.float32)).astype(
        jnp.bfloat16
    )
    grad_tokens = grad_sum1 + jnp.dot(grad_query, wq.T, preferred_element_type=jnp.float32)
    grad_tokens = grad_tokens + jnp.dot(grad_key, wk.T, preferred_element_type=jnp.float32)
    grad_tokens = grad_tokens + jnp.dot(grad_value, wv.T, preferred_element_type=jnp.float32)
    grad_tokens = grad_tokens + jnp.dot(grad_low_q, dq_mat.T, preferred_element_type=jnp.float32)
    grad_tokens = grad_tokens + jnp.dot(grad_low_v, dv_mat.T, preferred_element_type=jnp.float32)
    local_q = 2.0 * jnp.einsum("tr,td->rd", low_q, grad_query, preferred_element_type=jnp.float32)
    local_v = 2.0 * jnp.einsum("tr,td->rd", low_v, grad_value, preferred_element_type=jnp.float32)
    total_q, total_v = lax.psum((local_q, local_v), ("dp", "fsdp"))
    return (
        layer_out.reshape(row_count, length, width),
        grad_tokens.astype(jnp.bfloat16).reshape(row_count, length, width),
        total_q,
        total_v,
    )


def solution(mesh):
    placed = (
        P(("dp", "fsdp"), None, None),
        P(("dp", "fsdp"), None),
        P(("dp", "fsdp"), None),
        P(("dp", "fsdp"), None),
        P(("dp", "fsdp"), None),
        P(("dp", "fsdp"), None),
        P(("dp", "fsdp"), None),
        P(("dp", "fsdp"), None),
        P(("dp", "fsdp"), None),
        P(("dp", "fsdp"), None),
        P(),
        P(),
        P(),
        P(),
        P(),
        P(),
        P(("dp", "fsdp"), None, None),
    )
    return jax.shard_map(
        body,
        mesh=mesh,
        in_specs=placed,
        out_specs=(P(("dp", "fsdp"), None, None), P(("dp", "fsdp"), None, None), P(), P()),
        check_vma=False,
    )
```

profile of v0, /device:TPU:0, one launch (start us, length us, event | category | flops | bytes accessed | tf_op | source)
XLA Modules:
  0.0 558.4 jit_solution(10017231867190146173)
XLA Ops:
  11.2 43.6 %all-gather = bf16[32,24,8]{1,2,0:T(8,128)(2,1)S(1)} all-gather(bf16[1,24,8]{1,2,0:T(8,128)(2,1)} %bitcast.217), channel_id=1, replica_groups=mesh['dp'=8,'fsdp'=4] {'dp','fsdp'}, dimensions={0}, use_global_device_ids=true | all-gather | bytes 12672 | tf_op jit(solution)/shard_map/all_gather | solution.py:61
  55.0 37.1 %all-gather.1 = bf16[32,24,8]{1,2,0:T(8,128)(2,1)S(1)} all-gather(bf16[1,24,8]{1,2,0:T(8,128)(2,1)} %bitcast.218), channel_id=1, replica_groups=mesh['dp'=8,'fsdp'=4] {'dp','fsdp'}, dimensions={0}, use_global_device_ids=true | all-gather | bytes 12672 | tf_op jit(solution)/shard_map/all_gather | solution.py:60
  108.5 15.2 %all-gather.11.cloned.1.call-done = bf16[768,768]{1,0:T(8,128)(2,1)} async-done(((bf16[24,768]{1,0:T(8,128)(2,1)}), bf16[768,768]{1,0:T(8,128)(2,1)}) %all-gather.11.cloned.1.call-update) | async-done | bytes 1179664 | tf_op jit(solution)/shard_map/all_gather | solution.py:54
  134.0 45.7 %all-gather.13.cloned.1.call-done = bf16[768,768]{1,0:T(8,128)(2,1)} async-done(((bf16[24,768]{1,0:T(8,128)(2,1)}), bf16[768,768]{1,0:T(8,128)(2,1)}) %all-gather.13.cloned.1.call-update) | async-done | bytes 1179664 | tf_op jit(solution)/shard_map/all_gather | solution.py:55
  179.7 3.8 convolution_convert_fusion.1
  190.7 20.9 %while.26 = (s32[]{:T(128)}, bf16[2,512,12,64]{1,3,2,0:T(8,128)(2,1)}, f32[2,12,512,1]{2,1,3,0:T(8,128)S(1)}, bf16[2,512,12,64]{1,3,2,0:T(8,128)(2,1)}, s32[2,51...) while((s32[]{:T(128)}, ...), condition=%wide.region_3.4_spmd, body=%wide.region_0.3_spmd.sunk | while | flops 843704320 | bytes 42172508 | solution.py:90
  195.8 5.4 fusion.162
  206.2 5.4 fusion.162
  211.6 3.0 copy.65
  216.2 19.4 %all-gather.15.cloned.1.call-done = bf16[768,768]{1,0:T(8,128)(2,1)} async-done(((bf16[24,768]{1,0:T(8,128)(2,1)}), bf16[768,768]{1,0:T(8,128)(2,1)}) %all-gather.15.cloned.1.call-update) | async-done | bytes 1179664 | tf_op jit(solution)/shard_map/all_gather | solution.py:57
  235.6 5.4 fusion.89
  243.4 57.5 %all-gather.17.cloned.1.call-done = bf16[768,3072]{1,0:T(8,128)(2,1)} async-done(((bf16[24,3072]{1,0:T(8,128)(2,1)}), bf16[768,3072]{1,0:T(8,128)(2,1)}) %all-gather.17.cloned.1.call-update) | async-done | bytes 4718608 | tf_op jit(solution)/shard_map/all_gather | solution.py:58
  300.9 36.5 %fusion.57 = (f32[1024,3072]{1,0:T(8,128)}, f32[1024,3072]{1,0:T(8,128)}) fusion(bf16[768,3072]{1,0:T(8,128)(2,1)} %all-gather.17.cloned.1.call-done, f32[1024,768]{1,0:T(8,128)} %get-tuple-element.197, f32[768]{0:T(1024)S(1)} %copy-done.39, f32[768]{0:T(1024)S(1)} %copy-done.40, f32[1024]{0:T(1024)S(1)} %add_rsqrt_fusion.1, ...), kind=kOutput, calls=%fused_computation.65 | convolution fusion | flops 5030805504 | bytes 33044480 | tf_op jit(solution)/shard_map/dot_general | solution.py:98
  337.4 28.7 %all-gather.19.cloned.1.call-done = bf16[3072,768]{1,0:T(8,128)(2,1)} async-done(((bf16[96,768]{1,0:T(8,128)(2,1)}), bf16[3072,768]{1,0:T(8,128)(2,1)}) %all-gather.19.cloned.1.call-update) | async-done | bytes 4718608 | tf_op jit(solution)/shard_map/all_gather | solution.py:59
  366.1 15.6 %fusion.90 = (f32[1024]{0:T(1024)S(1)}, f32[1024,768]{1,0:T(8,128)S(1)}) fusion(bf16[3072,768]{1,0:T(8,128)(2,1)} %all-gather.19.cloned.1.call-done, f32[1024,3072]{1,0:T(8,128)} %get-tuple-element.198, f32[1024,3072]{1,0:T(8,128)} %get-tuple-element.199, f32[768]{0:T(1024)S(1)} %copy-done.39, f32[768]{0:T(1024)S(1)} %copy-done.40, ...), kind=kOutput, calls=%fused_computation.140 | convolution fusion | flops 4845992960 | bytes 36194304 | tf_op jit(solution)/shard_map/dot_general | solution.py:100
  384.0 3.1 subtract_multiply_fusion.1
  387.1 22.7 %fusion.88 = (f32[1024]{0:T(1024)S(1)}, f32[1024]{0:T(1024)S(1)}, f32[1024,768]{1,0:T(8,128)}) fusion(f32[1024]{0:T(1024)S(1)} %add_rsqrt_fusion.1, f32[1024,768]{1,0:T(8,128)} %get-tuple-element.197, f32[1024]{0:T(1024)S(1)} %broadcast_multiply_fusion.4, f32[768]{0:T(1024)S(1)} %copy-done.40, f32[1024,768]{1,0:T(8,128)} %get-tuple-element.194, ...), kind=kOutput, calls=%fused_computation.138 | convolution fusion | flops 9714006016 | bytes 44059648 | tf_op jit(solution)/shard_map/dot_general | solution.py:121
  409.9 6.1 %convolution_convert_fusion = bf16[1024,768]{1,0:T(8,128)(2,1)} fusion(bf16[768,768]{1,0:T(8,128)(2,1)} %all-gather.15.cloned.1.call-done, f32[1024,768]{1,0:T(8,128)} %get-tuple-element.202, f32[1024,768]{1,0:T(8,128)} %get-tuple-element.197, f32[1024]{0:T(1024)S(1)} %get-tuple-element.203, f32[1024]{0:T(1024)S(1)} %get-tuple-element.204, ...), kind=kOutput, calls=%fused_computation.103 | convolution fusion | flops 1214251008 | bytes 9060352 | tf_op jit(solution)/shard_map/dot_general | solution.py:124
  418.6 3.8 reshape.190
  429.3 48.3 %while.27 = (s32[]{:T(128)}, bf16[2,512,12,64]{1,3,2,0:T(8,128)(2,1)}, bf16[2,512,12,64]{1,3,2,0:T(8,128)(2,1)}, bf16[2,512,12,64]{1,3,2,0:T(8,128)(2,1)}, bf16[...) while((s32[]{:T(128)}, ...), condition=%wide.region_14.15_spmd, body=%wide.region_12.14_spmd.sunk | while | flops 2062673920 | bytes 147524944 | solution.py:153
  431.4 6.7 %multiply_reduce_fusion.7 = (f32[12,512]{1,0:T(8,128)S(1)}, f32[12,512,512]{1,2,0:T(8,128)}) fusion(f32[12,512,512]{1,2,0:T(8,128)S(1)} %fusion.171, f32[12,512]{1,0:T(8,128)S(1)} %dynamic-slice_bitcast_fusion.2, pred[512,512]{0,1:T(8,128)(4,1)S(1)} %broadcast_compare_fusion.5, bf16[2,512,12,64]{1,3,2,0:T(8,128)(2,1)S(1)} %copy-done.1, ...), kind=kOutput, calls=%fused_computation.24.clone.1 | convolution fusion | flops 418375680 | bytes 27059200 | tf_op jit(solution)/shard_map/while/body/eval_jaxpr/qhd,khd->hqk/dot_general | solution.py:136
  438.2 6.8 %multiply_convert_fusion.8 = bf16[12,512,512]{1,2,0:T(8,128)(2,1)S(1)} fusion(f32[12,512,512]{1,2,0:T(8,128)} %get-tuple-element.315, f32[12,512,512]{1,2,0:T(8,128)S(1)} %fusion.171, f32[12,512]{1,0:T(8,128)S(1)} %get-tuple-element.316, f32[12,512]{1,0:T(8,128)S(1)} %dynamic-slice_bitcast_fusion.2, pred[512,512]{0,1:T(8,128)(4,1)S(1)} %broadcast_compare_fusion.5), kind=kLoop, calls=%fused_computation.23.clone.1 | loop fusion | flops 18874368 | bytes 31768576 | tf_op jit(solution)/shard_map/while/body/eval_jaxpr/convert_element_type | solution.py:138
  449.4 4.0 fusion.174
  455.5 6.7 %multiply_reduce_fusion.7 = (f32[12,512]{1,0:T(8,128)S(1)}, f32[12,512,512]{1,2,0:T(8,128)}) fusion(f32[12,512,512]{1,2,0:T(8,128)S(1)} %fusion.171, f32[12,512]{1,0:T(8,128)S(1)} %dynamic-slice_bitcast_fusion.2, pred[512,512]{0,1:T(8,128)(4,1)S(1)} %broadcast_compare_fusion.5, bf16[2,512,12,64]{1,3,2,0:T(8,128)(2,1)S(1)} %copy-done.1, ...), kind=kOutput, calls=%fused_computation.24.clone.1 | convolution fusion | flops 418375680 | bytes 27059200 | tf_op jit(solution)/shard_map/while/body/eval_jaxpr/qhd,khd->hqk/dot_general | solution.py:136
  462.2 6.8 %multiply_convert_fusion.8 = bf16[12,512,512]{1,2,0:T(8,128)(2,1)S(1)} fusion(f32[12,512,512]{1,2,0:T(8,128)} %get-tuple-element.315, f32[12,512,512]{1,2,0:T(8,128)S(1)} %fusion.171, f32[12,512]{1,0:T(8,128)S(1)} %get-tuple-element.316, f32[12,512]{1,0:T(8,128)S(1)} %dynamic-slice_bitcast_fusion.2, pred[512,512]{0,1:T(8,128)(4,1)S(1)} %broadcast_compare_fusion.5), kind=kLoop, calls=%fused_computation.23.clone.1 | loop fusion | flops 18874368 | bytes 31768576 | tf_op jit(solution)/shard_map/while/body/eval_jaxpr/convert_element_type | solution.py:138
  473.5 4.0 fusion.174
  477.6 3.0 copy.71
  490.4 40.9 %all-reduce = (f32[8,768]{1,0:T(8,128)}, f32[8,768]{1,0:T(8,128)}) all-reduce(f32[8,768]{1,0:T(8,128)S(1)} %convolution_multiply_fusion.3, f32[8,768]{1,0:T(8,128)S(1)} %convolution_multiply_fusion.2), channel_id=1, replica_groups=mesh['dp'=8,'fsdp'=4] {'dp','fsdp'}, use_global_device_ids=true, to_apply=%region_15.16 | all-reduce | flops 12288 | bytes 98304 | tf_op jit(solution)/shard_map/psum | solution.py:172
  531.3 4.5 fusion.93
  535.8 3.2 fusion.95
  539.1 3.1 fusion.94
  542.3 8.9 %add_convert_fusion.2 = bf16[1024,768]{1,0:T(8,128)(2,1)} fusion(f32[1024,768]{1,0:T(8,128)} %fusion.79, f32[1024,768]{1,0:T(8,128)} %fusion.95, f32[1024,768]{1,0:T(8,128)} %fusion.94, f32[1024,768]{1,0:T(8,128)} %fusion.93, bf16[768,8]{0,1:T(8,128)(2,1)S(1)} %copy-done.19, bf16[1024,768]{0,1:T(8,128)(2,1)S(1)} %bitcast.196, ...), kind=kOutput, calls=%fused_computation.85 | convolution fusion | flops 34619392 | bytes 22061056 | tf_op jit(solution)/shard_map/dot_general | solution.py:169
  (178 shorter events, 86.0 us)
Async XLA Ops:
  7.2 119.3 %copy-start = (bf16[8,768]{1,0:T(8,128)(2,1)S(1)}, bf16[8,768]{1,0:T(8,128)(2,1)}, u32[]{:S(2)}) copy-start(bf16[8,768]{1,0:T(8,128)(2,1)} %param.31) | copy-start | bytes 36868
  7.2 89.9 %copy-start.6 = (bf16[2,512,768]{2,1,0:T(8,128)(2,1)S(1)}, bf16[2,512,768]{2,1,0:T(8,128)(2,1)}, u32[]{:S(2)}) copy-start(bf16[2,512,768]{2,1,0:T(8,128)(2,1)} %param.21) | copy-start | bytes 4718596
  7.2 88.9 %copy-start.25 = (f32[768]{0:T(1024)S(1)}, f32[768]{0:T(1024)}, u32[]{:S(2)}) copy-start(f32[768]{0:T(1024)} %param.35) | copy-start | bytes 9220
  7.2 88.9 %copy-start.4 = (bf16[2,512,768]{2,1,0:T(8,128)(2,1)S(1)}, bf16[2,512,768]{2,1,0:T(8,128)(2,1)}, u32[]{:S(2)}) copy-start(bf16[2,512,768]{2,1,0:T(8,128)(2,1)} %param.37) | copy-start | bytes 4718596
  7.2 89.9 %all-gather.9.cloned.1.call-start = ((), (), s32[]{:S(2)}) async-start(), calls=%async_computation | async-start | bytes 1216512 | tf_op jit(solution)/shard_map/all_gather | solution.py:56
  8.0 115.8 %all-gather.11.cloned.1.call-start = ((), (), s32[]{:S(2)}) async-start(), calls=%async_computation.1 | async-start | bytes 1216512 | tf_op jit(solution)/shard_map/all_gather | solution.py:54
  8.7 171.0 %all-gather.13.cloned.1.call-start = ((), (), s32[]{:S(2)}) async-start(), calls=%async_computation.2 | async-start | bytes 1216512 | tf_op jit(solution)/shard_map/all_gather | solution.py:55
  9.4 226.1 %all-gather.15.cloned.1.call-start = ((), (), s32[]{:S(2)}) async-start(), calls=%async_computation.3 | async-start | bytes 1216512 | tf_op jit(solution)/shard_map/all_gather | solution.py:57
  10.0 290.9 %all-gather.17.cloned.1.call-start = ((), (), s32[]{:S(2)}) async-start(), calls=%async_computation.4 | async-start | bytes 4866048 | tf_op jit(solution)/shard_map/all_gather | solution.py:58
  10.6 355.5 %all-gather.19.cloned.1.call-start = ((), (), s32[]{:S(2)}) async-start(), calls=%async_computation.5 | async-start | bytes 4866048 | tf_op jit(solution)/shard_map/all_gather | solution.py:59
  55.0 44.8 %copy-start.18 = (bf16[768,8]{0,1:T(8,128)(2,1)}, bf16[768,8]{0,1:T(8,128)(2,1)S(1)}, u32[]{:S(2)}) copy-start(bf16[768,8]{0,1:T(8,128)(2,1)S(1)} %reshape.197) | copy-start | bytes 36868
  92.2 7.6 %copy-start.20 = (bf16[768,8]{0,1:T(8,128)(2,1)}, bf16[768,8]{0,1:T(8,128)(2,1)S(1)}, u32[]{:S(2)}) copy-start(bf16[768,8]{0,1:T(8,128)(2,1)S(1)} %reshape.199) | copy-start | bytes 36868
  94.1 5.7 %copy-start.14 = (bf16[1024,8]{0,1:T(8,128)(2,1)}, bf16[1024,8]{0,1:T(8,128)(2,1)S(1)}, u32[]{:S(2)}) copy-start(bf16[1024,8]{0,1:T(8,128)(2,1)S(1)} %convolution_convert_fusion.3) | copy-start | bytes 49156
  96.1 30.4 %copy-start.16 = (bf16[1024,8]{0,1:T(8,128)(2,1)}, bf16[1024,8]{0,1:T(8,128)(2,1)S(1)}, u32[]{:S(2)}) copy-start(bf16[1024,8]{0,1:T(8,128)(2,1)S(1)} %convolution_convert_fusion.2) | copy-start | bytes 49156
  241.0 59.9 %copy-start.39 = (f32[768]{0:T(1024)S(1)}, f32[768]{0:T(1024)}, u32[]{:S(2)}) copy-start(f32[768]{0:T(1024)} %param.34) | copy-start | bytes 9220
  241.0 59.9 %copy-start.40 = (f32[768]{0:T(1024)S(1)}, f32[768]{0:T(1024)}, u32[]{:S(2)}) copy-start(f32[768]{0:T(1024)} %param.33) | copy-start | bytes 9220
  241.0 168.9 %copy-start.27 = (f32[1024]{0:T(1024)}, f32[1024]{0:T(1024)S(1)}, u32[]{:S(2)}) copy-start(f32[1024]{0:T(1024)S(1)} %broadcast_multiply_fusion.4) | copy-start | bytes 12292
  243.4 166.5 %copy-start.29 = (f32[1024]{0:T(1024)}, f32[1024]{0:T(1024)S(1)}, u32[]{:S(2)}) copy-start(f32[1024]{0:T(1024)S(1)} %add_rsqrt_fusion.1) | copy-start | bytes 12292
  409.8 6.1 %copy-start.32 = (f32[1024]{0:T(1024)}, f32[1024]{0:T(1024)S(1)}, u32[]{:S(2)}) copy-start(f32[1024]{0:T(1024)S(1)} %get-tuple-element.203) | copy-start | bytes 12292
  409.8 6.1 %copy-start.34 = (f32[1024]{0:T(1024)}, f32[1024]{0:T(1024)S(1)}, u32[]{:S(2)}) copy-start(f32[1024]{0:T(1024)S(1)} %get-tuple-element.204) | copy-start | bytes 12292
  438.2 6.8 %copy-start.9 = (bf16[2,512,12,64]{1,3,2,0:T(8,128)(2,1)S(1)}, bf16[2,512,12,64]{1,3,2,0:T(8,128)(2,1)}, u32[]{:S(2)}) copy-start(bf16[2,512,12,64]{1,3,2,0:T(8,128)(2,1)} %get-tuple-element.354) | copy-start | bytes 4718596 | tf_op jit(solution)/shard_map/while
  462.2 6.8 %copy-start.9 = (bf16[2,512,12,64]{1,3,2,0:T(8,128)(2,1)S(1)}, bf16[2,512,12,64]{1,3,2,0:T(8,128)(2,1)}, u32[]{:S(2)}) copy-start(bf16[2,512,12,64]{1,3,2,0:T(8,128)(2,1)} %get-tuple-element.354) | copy-start | bytes 4718596 | tf_op jit(solution)/shard_map/while
  477.6 3.5 copy-start.17
  531.3 4.5 copy-start.37
  535.8 3.2 copy-start.13
  535.8 3.2 copy-start.38
  539.0 3.2 copy-start.19
  539.0 3.2 copy-start.24
  539.1 3.2 copy-start.28
  539.1 3.2 copy-start.30
  539.1 3.2 copy-start.33
  539.1 3.2 copy-start.35
  (22 other events, 41.5 us)
Sparse Core Ops, SparseCore 0:
  11.0 56.7 all-gather.8
  70.7 53.0 all-gather.10
  126.7 53.0 all-gather.12
  182.5 53.0 all-gather.14
  238.3 62.5 all-gather.16
  303.6 62.4 all-gather.18
where the time goes:
time: 566 us; the launch traced here: 558 us
  matrix products  173 us (31%)
  waiting for transfers between devices  170 us (30%)
  blocking collectives  122 us (22%)
  local copies, waits for them, and re-layouts  51.2 us (9%)
  other arithmetic  27 us (5%)
  between operations  15 us (3%)
    all_gather x1, waiting for transfers between devices, body(): lax.all_gather(w_inner, ('dp', 'fsdp'), axis=0, tiled=True)  57.5 us
    all_gather x1, waiting for transfers between devices, body(): lax.all_gather(w_key, ('dp', 'fsdp'), axis=0, tiled=True)  45.7 us
    all_gather x1, blocking collectives, body(): lax.all_gather(down_value, ('dp', 'fsdp'), axis=0, tiled=True)  43.6 us
    psum x1, blocking collectives, body(): total_q, total_v = lax.psum((local_q, local_v), ('dp', 'fsdp'))  40.9 us
    all_gather x1, blocking collectives, body(): lax.all_gather(down_query, ('dp', 'fsdp'), axis=0, tiled=True)  37.1 us
    dot_general x1, matrix products, body(): inner = jnp.dot(hidden_low, win, preferred_element_type=jnp.float32)  36.5 us
    all_gather x1, waiting for transfers between devices, body(): lax.all_gather(w_outer, ('dp', 'fsdp'), axis=0, tiled=True)  28.7 us
    dot_general x1, matrix products, body(): jnp.dot(grad_inner, win.T, preferred_element_type=jnp.float32)  22.7 us
  transfers between devices with their start and end apart: 6, of which 5 were waited for; matrix products, arithmetic and copies ran while one was open for 19% of the time, Pallas kernels for 0%

commit v1 on v0

--- a/solution.py
+++ b/solution.py
@@ -50,8 +50,23 @@
 ):
     row_count, length, width = tokens.shape
     count = row_count * length
+
+    def lift_view(v0, dimension_no=0):
+        moved, formed = (lax.axis_size(("dp", "fsdp")), lax.axis_index(("dp", "fsdp")))
+        block_last, d_next = (v0, 1)
+        while d_next < moved:
+            history = []
+            for m in range(moved):
+                history.append((m, m ^ d_next))
+            r_now = lax.ppermute(block_last, ("dp", "fsdp"), perm=history)
+            value_now = jnp.concatenate([block_last, r_now], axis=dimension_no)
+            y2 = jnp.concatenate([r_now, block_last], axis=dimension_no)
+            block_last = jnp.where(formed & d_next == 0, value_now, y2)
+            d_next = 2 * d_next
+        return block_last
+
     whole = (
-        lax.all_gather(w_query, ("dp", "fsdp"), axis=0, tiled=True),
+        lift_view(w_query),
         lax.all_gather(w_key, ("dp", "fsdp"), axis=0, tiled=True),
         lax.all_gather(w_value, ("dp", "fsdp"), axis=0, tiled=True),
         lax.all_gather(w_output, ("dp", "fsdp"), axis=0, tiled=True),

time: 566 us -> 515 us (0.910)
  waiting for transfers between devices: 170 us -> 99.8 us
  blocking collectives: 122 us -> 131 us
  starting transfers between devices: 0.23 us -> 7.16 us
    all_gather x1, waiting for transfers between devices: 45.7 us -> 0.01 us  [body(): lax.all_gather(w_key, ('dp', 'fsdp'), axis=0, tiled=True)]
    all_gather x1, waiting for transfers between devices: 19.4 us -> 3.08 us  [body(): lax.all_gather(w_output, ('dp', 'fsdp'), axis=0, tiled=True)]
    all_gather x1, waiting for transfers between devices: 15.2 us -> 0.01 us  [body(): lax.all_gather(w_query, ('dp', 'fsdp'), axis=0, tiled=True)]
    ppermute x0 -> x5, waiting for transfers between devices: none -> 7.32 us  [lift_view(): r_now = lax.ppermute(block_last, ('dp', 'fsdp'), perm=history)]
    ppermute x0 -> x5, starting transfers between devices: none -> 6.93 us  [lift_view(): r_now = lax.ppermute(block_last, ('dp', 'fsdp'), perm=history)]
  transfers between devices with their start and end apart: 6 -> 11, of which waited for: 5 -> 6; matrix products, arithmetic and copies ran while one was open for 19% -> 46% of each run, Pallas kernels for 0% -> 0%
where the time goes in v1:
time: 515 us; the launch traced here: 506 us
  matrix products  170 us (33%)
  blocking collectives  131 us (25%)
  waiting for transfers between devices  99.8 us (19%)
  local copies, waits for them, and re-layouts  53.2 us (10%)
  other arithmetic  29.5 us (6%)
  between operations  15.1 us (3%)
  starting transfers between devices  7.16 us (1%)
    all_gather x1, waiting for transfers between devices, body(): lax.all_gather(w_inner, ('dp', 'fsdp'), axis=0, tiled=True)  57.4 us
    all_gather x1, blocking collectives, body(): lax.all_gather(down_value, ('dp', 'fsdp'), axis=0, tiled=True)  48.8 us
    all_gather x1, blocking collectives, body(): lax.all_gather(down_query, ('dp', 'fsdp'), axis=0, tiled=True)  41.4 us
    psum x1, blocking collectives, body(): total_q, total_v = lax.psum((local_q, local_v), ('dp', 'fsdp'))  40.9 us
    dot_general x1, matrix products, body(): inner = jnp.dot(hidden_low, win, preferred_element_type=jnp.float32)  36.5 us
    all_gather x1, waiting for transfers between devices, body(): lax.all_gather(w_outer, ('dp', 'fsdp'), axis=0, tiled=True)  28.8 us
    dot_general x1, matrix products, body(): jnp.dot(grad_inner, win.T, preferred_element_type=jnp.float32)  22.7 us
    dot_general x1, matrix products, body(): jnp.dot(active, wout, preferred_element_type=jnp.float32)  15.6 us
  transfers between devices with their start and end apart: 11, of which 6 were waited for; matrix products, arithmetic and copies ran while one was open for 46% of the time, Pallas kernels for 0%

profile of v1, /device:TPU:0, one launch (start us, length us, event | category | flops | bytes accessed | tf_op | source)
XLA Modules:
  0.0 506.3 jit_solution(8519195184965840696)
XLA Ops:
  20.5 3.6 collective-permute-done.2
  27.6 41.4 %all-gather.1 = bf16[32,24,8]{1,2,0:T(8,128)(2,1)S(1)} all-gather(bf16[1,24,8]{1,2,0:T(8,128)(2,1)} %bitcast.220), channel_id=1, replica_groups=mesh['dp'=8,'fsdp'=4] {'dp','fsdp'}, dimensions={0}, use_global_device_ids=true | all-gather | bytes 12672 | tf_op jit(solution)/shard_map/all_gather | solution.py:75
  70.0 48.8 %all-gather = bf16[32,24,8]{1,2,0:T(8,128)(2,1)S(1)} all-gather(bf16[1,24,8]{1,2,0:T(8,128)(2,1)S(1)} %bitcast.221), channel_id=1, replica_groups=mesh['dp'=8,'fsdp'=4] {'dp','fsdp'}, dimensions={0}, use_global_device_ids=true | all-gather | bytes 12672 | tf_op jit(solution)/shard_map/all_gather | solution.py:76
  136.2 3.8 reshape.185
  143.0 3.8 convolution_convert_fusion.1
  153.9 20.9 %while.26 = (s32[]{:T(128)}, bf16[2,512,12,64]{1,3,2,0:T(8,128)(2,1)}, f32[2,12,512,1]{2,1,3,0:T(8,128)S(1)}, bf16[2,512,12,64]{1,3,2,0:T(8,128)(2,1)}, s32[2,51...) while((s32[]{:T(128)}, ...), condition=%wide.region_3.4_spmd, body=%wide.region_0.3_spmd.sunk | while | flops 843704320 | bytes 42172508 | solution.py:105
  159.1 5.4 %fusion.169 = bf16[2,512,12,64]{1,3,2,0:T(8,128)(2,1)} fusion(bf16[2,512,12,64]{1,3,2,0:T(8,128)(2,1)} %get-tuple-element.326, s32[]{:T(128)} %get-tuple-element.325, f32[12,512,512]{1,2,0:T(8,128)S(1)} %get-tuple-element.303, f32[12,512]{1,0:T(8,128)S(1)} %fusion.168, f32[12,512]{1,0:T(8,128)S(1)} %get-tuple-element.304, ...), kind=kOutput, calls=%fused_computation.8.clone.1 | convolution fusion | flops 418775040 | bytes 14468096 | tf_op jit(solution)/shard_map/while/body/eval_jaxpr/hqk,khd->qhd/dot_general | solution.py:102
  169.4 5.4 %fusion.169 = bf16[2,512,12,64]{1,3,2,0:T(8,128)(2,1)} fusion(bf16[2,512,12,64]{1,3,2,0:T(8,128)(2,1)} %get-tuple-element.326, s32[]{:T(128)} %get-tuple-element.325, f32[12,512,512]{1,2,0:T(8,128)S(1)} %get-tuple-element.303, f32[12,512]{1,0:T(8,128)S(1)} %fusion.168, f32[12,512]{1,0:T(8,128)S(1)} %get-tuple-element.304, ...), kind=kOutput, calls=%fused_computation.8.clone.1 | convolution fusion | flops 418775040 | bytes 14468096 | tf_op jit(solution)/shard_map/while/body/eval_jaxpr/hqk,khd->qhd/dot_general | solution.py:102
  174.8 3.0 copy.68
  179.4 3.1 all-gather.13.cloned.1.call-done
  182.5 5.4 %fusion.97 = (f32[1024]{0:T(1024)S(1)}, f32[1024,768]{1,0:T(8,128)}) fusion(bf16[1024,768]{0,1:T(8,128)(2,1)} %bitcast.215, bf16[768,768]{1,0:T(8,128)(2,1)} %all-gather.13.cloned.1.call-done, bf16[1024,768]{1,0:T(8,128)(2,1)} %bitcast.203), kind=kOutput, calls=%fused_computation.152 | convolution fusion | flops 1210317824 | bytes 7475200 | tf_op jit(solution)/shard_map/dot_general | solution.py:107
  190.3 57.4 %all-gather.15.cloned.1.call-done = bf16[768,3072]{1,0:T(8,128)(2,1)} async-done(((bf16[24,3072]{1,0:T(8,128)(2,1)}), bf16[768,3072]{1,0:T(8,128)(2,1)}) %all-gather.15.cloned.1.call-update) | async-done | bytes 4718608 | tf_op jit(solution)/shard_map/all_gather | solution.py:73
  247.8 36.5 %fusion.57 = (f32[1024,3072]{1,0:T(8,128)}, f32[1024,3072]{1,0:T(8,128)}) fusion(bf16[768,3072]{1,0:T(8,128)(2,1)} %all-gather.15.cloned.1.call-done, f32[1024,768]{1,0:T(8,128)} %get-tuple-element.197, f32[768]{0:T(1024)S(1)} %copy-done.37, f32[768]{0:T(1024)S(1)} %copy-done.38, f32[1024]{0:T(1024)S(1)} %add_rsqrt_fusion.1, ...), kind=kOutput, calls=%fused_computation.65 | convolution fusion | flops 5030805504 | bytes 33044480 | tf_op jit(solution)/shard_map/dot_general | solution.py:113
  284.2 28.8 %all-gather.17.cloned.1.call-done = bf16[3072,768]{1,0:T(8,128)(2,1)} async-done(((bf16[96,768]{1,0:T(8,128)(2,1)}), bf16[3072,768]{1,0:T(8,128)(2,1)}) %all-gather.17.cloned.1.call-update) | async-done | bytes 4718608 | tf_op jit(solution)/shard_map/all_gather | solution.py:74
  313.0 15.6 %fusion.98 = (f32[1024]{0:T(1024)S(1)}, f32[1024,768]{1,0:T(8,128)S(1)}) fusion(bf16[3072,768]{1,0:T(8,128)(2,1)} %all-gather.17.cloned.1.call-done, f32[1024,3072]{1,0:T(8,128)} %get-tuple-element.198, f32[1024,3072]{1,0:T(8,128)} %get-tuple-element.199, f32[768]{0:T(1024)S(1)} %copy-done.37, f32[768]{0:T(1024)S(1)} %copy-done.38, ...), kind=kOutput, calls=%fused_computation.153 | convolution fusion | flops 4845992960 | bytes 36194304 | tf_op jit(solution)/shard_map/dot_general | solution.py:115
  330.9 3.1 subtract_multiply_fusion.1
  334.0 22.7 %fusion.96 = (f32[1024]{0:T(1024)S(1)}, f32[1024]{0:T(1024)S(1)}, f32[1024,768]{1,0:T(8,128)}) fusion(f32[1024]{0:T(1024)S(1)} %add_rsqrt_fusion.1, f32[1024,768]{1,0:T(8,128)} %get-tuple-element.197, f32[1024]{0:T(1024)S(1)} %broadcast_multiply_fusion.4, f32[768]{0:T(1024)S(1)} %copy-done.38, f32[1024,768]{1,0:T(8,128)} %get-tuple-element.194, ...), kind=kOutput, calls=%fused_computation.151 | convolution fusion | flops 9714006016 | bytes 44059648 | tf_op jit(solution)/shard_map/dot_general | solution.py:136
  356.8 6.1 %convolution_convert_fusion = bf16[1024,768]{1,0:T(8,128)(2,1)} fusion(bf16[768,768]{1,0:T(8,128)(2,1)} %all-gather.13.cloned.1.call-done, f32[1024,768]{1,0:T(8,128)} %get-tuple-element.202, f32[1024,768]{1,0:T(8,128)} %get-tuple-element.197, f32[1024]{0:T(1024)S(1)} %get-tuple-element.203, f32[1024]{0:T(1024)S(1)} %get-tuple-element.204, ...), kind=kOutput, calls=%fused_computation.104 | convolution fusion | flops 1214251008 | bytes 9060352 | tf_op jit(solution)/shard_map/dot_general | solution.py:139
  365.5 3.8 reshape.190
  376.2 48.3 %while.27 = (s32[]{:T(128)}, bf16[2,512,12,64]{1,3,2,0:T(8,128)(2,1)}, bf16[2,512,12,64]{1,3,2,0:T(8,128)(2,1)}, bf16[2,512,12,64]{1,3,2,0:T(8,128)(2,1)}, bf16[...) while((s32[]{:T(128)}, ...), condition=%wide.region_14.15_spmd, body=%wide.region_12.14_spmd.sunk | while | flops 2062673920 | bytes 147524944 | solution.py:168
  378.3 6.7 %multiply_reduce_fusion.7 = (f32[12,512]{1,0:T(8,128)S(1)}, f32[12,512,512]{1,2,0:T(8,128)}) fusion(f32[12,512,512]{1,2,0:T(8,128)S(1)} %fusion.178, f32[12,512]{1,0:T(8,128)S(1)} %dynamic-slice_bitcast_fusion.2, pred[512,512]{0,1:T(8,128)(4,1)S(1)} %broadcast_compare_fusion.5, bf16[2,512,12,64]{1,3,2,0:T(8,128)(2,1)S(1)} %copy-done.1, ...), kind=kOutput, calls=%fused_computation.24.clone.1 | convolution fusion | flops 418375680 | bytes 27059200 | tf_op jit(solution)/shard_map/while/body/eval_jaxpr/qhd,khd->hqk/dot_general | solution.py:151
  385.1 6.8 %multiply_convert_fusion.8 = bf16[12,512,512]{1,2,0:T(8,128)(2,1)S(1)} fusion(f32[12,512,512]{1,2,0:T(8,128)} %get-tuple-element.315, f32[12,512,512]{1,2,0:T(8,128)S(1)} %fusion.178, f32[12,512]{1,0:T(8,128)S(1)} %get-tuple-element.316, f32[12,512]{1,0:T(8,128)S(1)} %dynamic-slice_bitcast_fusion.2, pred[512,512]{0,1:T(8,128)(4,1)S(1)} %broadcast_compare_fusion.5), kind=kLoop, calls=%fused_computation.23.clone.1 | loop fusion | flops 18874368 | bytes 31768576 | tf_op jit(solution)/shard_map/while/body/eval_jaxpr/convert_element_type | solution.py:153
  396.3 4.0 fusion.181
  402.4 6.7 %multiply_reduce_fusion.7 = (f32[12,512]{1,0:T(8,128)S(1)}, f32[12,512,512]{1,2,0:T(8,128)}) fusion(f32[12,512,512]{1,2,0:T(8,128)S(1)} %fusion.178, f32[12,512]{1,0:T(8,128)S(1)} %dynamic-slice_bitcast_fusion.2, pred[512,512]{0,1:T(8,128)(4,1)S(1)} %broadcast_compare_fusion.5, bf16[2,512,12,64]{1,3,2,0:T(8,128)(2,1)S(1)} %copy-done.1, ...), kind=kOutput, calls=%fused_computation.24.clone.1 | convolution fusion | flops 418375680 | bytes 27059200 | tf_op jit(solution)/shard_map/while/body/eval_jaxpr/qhd,khd->hqk/dot_general | solution.py:151
  409.1 6.8 %multiply_convert_fusion.8 = bf16[12,512,512]{1,2,0:T(8,128)(2,1)S(1)} fusion(f32[12,512,512]{1,2,0:T(8,128)} %get-tuple-element.315, f32[12,512,512]{1,2,0:T(8,128)S(1)} %fusion.178, f32[12,512]{1,0:T(8,128)S(1)} %get-tuple-element.316, f32[12,512]{1,0:T(8,128)S(1)} %dynamic-slice_bitcast_fusion.2, pred[512,512]{0,1:T(8,128)(4,1)S(1)} %broadcast_compare_fusion.5), kind=kLoop, calls=%fused_computation.23.clone.1 | loop fusion | flops 18874368 | bytes 31768576 | tf_op jit(solution)/shard_map/while/body/eval_jaxpr/convert_element_type | solution.py:153
  420.3 4.0 fusion.181
  424.5 3.1 copy.76
  434.4 40.9 %all-reduce = (f32[8,768]{1,0:T(8,128)}, f32[8,768]{1,0:T(8,128)}) all-reduce(f32[8,768]{1,0:T(8,128)S(1)} %convolution_multiply_fusion.3, f32[8,768]{1,0:T(8,128)S(1)} %convolution_multiply_fusion.2), channel_id=1, replica_groups=mesh['dp'=8,'fsdp'=4] {'dp','fsdp'}, use_global_device_ids=true, to_apply=%region_15.16 | all-reduce | flops 12288 | bytes 98304 | tf_op jit(solution)/shard_map/psum | solution.py:187
  477.9 4.4 fusion.103
  482.3 4.6 fusion.101
  487.0 3.1 fusion.102
  490.1 8.9 %add_convert_fusion.2 = bf16[1024,768]{1,0:T(8,128)(2,1)} fusion(f32[1024,768]{1,0:T(8,128)} %fusion.86, f32[1024,768]{1,0:T(8,128)} %fusion.103, f32[1024,768]{1,0:T(8,128)} %fusion.102, f32[1024,768]{1,0:T(8,128)} %fusion.101, bf16[768,8]{0,1:T(8,128)(2,1)S(1)} %copy-done.20, bf16[1024,768]{0,1:T(8,128)(2,1)S(1)} %bitcast.199, ...), kind=kOutput, calls=%fused_computation.87 | convolution fusion | flops 34619392 | bytes 22061056 | tf_op jit(solution)/shard_map/dot_general | solution.py:184
  (188 shorter events, 92.6 us)
Async XLA Ops:
  7.2 112.9 %copy-start = (bf16[8,768]{1,0:T(8,128)(2,1)S(1)}, bf16[8,768]{1,0:T(8,128)(2,1)}, u32[]{:S(2)}) copy-start(bf16[8,768]{1,0:T(8,128)(2,1)} %param.31) | copy-start | bytes 36868
  7.2 62.0 %copy-start.5 = (bf16[2,512,768]{2,1,0:T(8,128)(2,1)S(1)}, bf16[2,512,768]{2,1,0:T(8,128)(2,1)}, u32[]{:S(2)}) copy-start(bf16[2,512,768]{2,1,0:T(8,128)(2,1)} %param.21) | copy-start | bytes 4718596
  7.2 62.8 %copy-start.35 = (bf16[24,8]{0,1:T(8,128)(2,1)S(1)}, bf16[24,8]{0,1:T(8,128)(2,1)}, u32[]{:S(2)}) copy-start(bf16[24,8]{0,1:T(8,128)(2,1)} %param.30) | copy-start | bytes 1156
  7.2 122.0 %all-gather.9.cloned.1.call-start = ((), (), s32[]{:S(2)}) async-start(), calls=%async_computation | async-start | bytes 1216512 | tf_op jit(solution)/shard_map/all_gather | solution.py:71
  7.9 135.0 %all-gather.11.cloned.1.call-start = ((), (), s32[]{:S(2)}) async-start(), calls=%async_computation.1 | async-start | bytes 1216512 | tf_op jit(solution)/shard_map/all_gather | solution.py:70
  8.7 173.8 %all-gather.13.cloned.1.call-start = ((), (), s32[]{:S(2)}) async-start(), calls=%async_computation.2 | async-start | bytes 1216512 | tf_op jit(solution)/shard_map/all_gather | solution.py:72
  9.4 238.3 %all-gather.15.cloned.1.call-start = ((), (), s32[]{:S(2)}) async-start(), calls=%async_computation.3 | async-start | bytes 4866048 | tf_op jit(solution)/shard_map/all_gather | solution.py:73
  10.0 303.0 %all-gather.17.cloned.1.call-start = ((), (), s32[]{:S(2)}) async-start(), calls=%async_computation.4 | async-start | bytes 4866048 | tf_op jit(solution)/shard_map/all_gather | solution.py:74
  10.6 471.7 %all-gather.19.cloned.1.call-start = ((), (), s32[]{:S(2)}) async-start(), calls=%async_computation.5 | async-start | bytes 1216512 | tf_op jit(solution)/shard_map/all_gather | solution.py:119
  10.6 1.6 collective-permute-start
  13.1 5.5 %collective-permute-start.1 = (bf16[48,768]{1,0:T(8,128)(2,1)S(1)}, bf16[48,768]{1,0:T(8,128)(2,1)S(1)}, u32[]{:S(2)}, u32[]{:S(2)}) collective-permute-start(bf16[48,768]{1,0:T(8,128)(2,1)S(1)} %maximum_select_fusion.5), channel_id=1, source_target_pairs={{0,2},{1,3},{2,0},{3,1},{4,6},{5,7},{6,4},{7,5},{8,10},{9,11},{10,... | collective-permute-start | bytes 221192 | tf_op jit(solution)/shard_map/ppermute | solution.py:61
  18.6 5.5 %collective-permute-start.2 = (bf16[96,768]{1,0:T(8,128)(2,1)S(1)}, bf16[96,768]{1,0:T(8,128)(2,1)S(1)}, u32[]{:S(2)}, u32[]{:S(2)}) collective-permute-start(bf16[96,768]{1,0:T(8,128)(2,1)S(1)} %maximum_select_fusion.4), channel_id=1, source_target_pairs={{0,4},{1,5},{2,6},{3,7},{4,0},{5,1},{6,2},{7,3},{8,12},{9,13},{10,... | collective-permute-start | bytes 442376 | tf_op jit(solution)/shard_map/ppermute | solution.py:61
  24.2 45.5 %collective-permute-start.3 = (bf16[192,768]{1,0:T(8,128)(2,1)S(1)}, bf16[192,768]{1,0:T(8,128)(2,1)S(1)}, u32[]{:S(2)}, u32[]{:S(2)}) collective-permute-start(bf16[192,768]{1,0:T(8,128)(2,1)S(1)} %maximum_select_fusion.3), channel_id=1, source_target_pairs={{0,8},{1,9},{2,10},{3,11},{4,12},{5,13},{6,14},{7,15},{8,0},{9,1},... | collective-permute-start | bytes 884744 | tf_op jit(solution)/shard_map/ppermute | solution.py:61
  69.7 53.6 %copy-start.13 = (bf16[1024,8]{0,1:T(8,128)(2,1)}, bf16[1024,8]{0,1:T(8,128)(2,1)S(1)}, u32[]{:S(2)}) copy-start(bf16[1024,8]{0,1:T(8,128)(2,1)S(1)} %convolution_convert_fusion.2) | copy-start | bytes 49156
  69.9 50.8 %collective-permute-start.4 = (bf16[384,768]{1,0:T(8,128)(2,1)S(1)}, bf16[384,768]{1,0:T(8,128)(2,1)S(1)}, u32[]{:S(2)}, u32[]{:S(2)}) collective-permute-start(bf16[384,768]{1,0:T(8,128)(2,1)S(1)} %maximum_select_fusion.2), channel_id=1, source_target_pairs={{0,16},{1,17},{2,18},{3,19},{4,20},{5,21},{6,22},{7,23},{8,24},{9,... | collective-permute-start | bytes 1769480 | tf_op jit(solution)/shard_map/ppermute | solution.py:61
  118.9 4.4 copy-start.19
  120.0 11.8 %copy-start.15 = (bf16[1024,8]{0,1:T(8,128)(2,1)}, bf16[1024,8]{0,1:T(8,128)(2,1)S(1)}, u32[]{:S(2)}) copy-start(bf16[1024,8]{0,1:T(8,128)(2,1)S(1)} %convolution_convert_fusion.3) | copy-start | bytes 49156
  187.9 59.9 %copy-start.37 = (f32[768]{0:T(1024)S(1)}, f32[768]{0:T(1024)}, u32[]{:S(2)}) copy-start(f32[768]{0:T(1024)} %param.34) | copy-start | bytes 9220
  187.9 59.9 %copy-start.38 = (f32[768]{0:T(1024)S(1)}, f32[768]{0:T(1024)}, u32[]{:S(2)}) copy-start(f32[768]{0:T(1024)} %param.33) | copy-start | bytes 9220
  187.9 168.9 %copy-start.25 = (f32[1024]{0:T(1024)}, f32[1024]{0:T(1024)S(1)}, u32[]{:S(2)}) copy-start(f32[1024]{0:T(1024)S(1)} %broadcast_multiply_fusion.4) | copy-start | bytes 12292
  190.3 166.5 %copy-start.27 = (f32[1024]{0:T(1024)}, f32[1024]{0:T(1024)S(1)}, u32[]{:S(2)}) copy-start(f32[1024]{0:T(1024)S(1)} %add_rsqrt_fusion.1) | copy-start | bytes 12292
  356.7 6.1 %copy-start.30 = (f32[1024]{0:T(1024)}, f32[1024]{0:T(1024)S(1)}, u32[]{:S(2)}) copy-start(f32[1024]{0:T(1024)S(1)} %get-tuple-element.203) | copy-start | bytes 12292
  356.7 6.1 %copy-start.32 = (f32[1024]{0:T(1024)}, f32[1024]{0:T(1024)S(1)}, u32[]{:S(2)}) copy-start(f32[1024]{0:T(1024)S(1)} %get-tuple-element.204) | copy-start | bytes 12292
  385.1 6.8 %copy-start.9 = (bf16[2,512,12,64]{1,3,2,0:T(8,128)(2,1)S(1)}, bf16[2,512,12,64]{1,3,2,0:T(8,128)(2,1)}, u32[]{:S(2)}) copy-start(bf16[2,512,12,64]{1,3,2,0:T(8,128)(2,1)} %get-tuple-element.354) | copy-start | bytes 4718596 | tf_op jit(solution)/shard_map/while
  409.1 6.8 %copy-start.9 = (bf16[2,512,12,64]{1,3,2,0:T(8,128)(2,1)S(1)}, bf16[2,512,12,64]{1,3,2,0:T(8,128)(2,1)}, u32[]{:S(2)}) copy-start(bf16[2,512,12,64]{1,3,2,0:T(8,128)(2,1)} %get-tuple-element.354) | copy-start | bytes 4718596 | tf_op jit(solution)/shard_map/while
  424.5 3.6 copy-start.8
  430.1 3.2 copy-start.16
  431.8 43.5 %copy-start.18 = (bf16[768,8]{0,1:T(8,128)(2,1)S(1)}, bf16[768,8]{0,1:T(8,128)(2,1)}, u32[]{:S(2)}) copy-start(bf16[768,8]{0,1:T(8,128)(2,1)} %copy-done.17) | copy-start | bytes 36868
  482.3 4.6 copy-start.12
  482.3 4.6 copy-start.36
  486.9 3.2 copy-start.20
  486.9 3.2 copy-start.23
  (25 other events, 51.7 us)
Sparse Core Ops, SparseCore 0:
  10.9 56.8 all-gather.8
  70.8 55.6 all-gather.10
  129.4 53.0 all-gather.12
  185.3 62.4 all-gather.14
  250.5 62.4 all-gather.16
  315.7 52.8 all-gather.18
